TPU v7x, 128 devices: a whole 4x4x4 slice. The times are simulated.
128 devices in a mesh: snap: 4 (over z_lo, core), pts: 32 (over z_hi, x, y).
Axes of the slice: x: 4, y: 4, z: 4 (z_hi: 2, z_lo: 2; z = z_hi * 2 + z_lo), core: 2. Of those that a mesh axis runs over, the one named last changes fastest.
Arguments:
- strains: bfloat16 [6, 512, 131072], P(None, 'snap', 'pts'), may hold values from -3 to 3
- moduli: float32 [2, 131072], P(None, 'pts'), may hold values from 0.5 to 2
- range_test: bfloat16 [131072, 256], P('pts'), may hold values from -0.015625 to 0.015625
- corange_test: bfloat16 [256, 512], replicated, may hold values from -0.25 to 0.25
- core_left: float32 [512, 512], P(None, 'snap'), may hold values from -0.25 to 0.25
- core_right: bfloat16 [512, 131072], P(None, 'pts'), may hold values from -0.015625 to 0.015625
Outputs:
- range_sketch: float32 [512, 256], P('snap')
- corange_sketch: float32 [256, 131072], P('snap', 'pts')
- core_sketch: float32 [512, 512], replicated
All inputs are finite; a program needn't handle non-finite values.
Results may differ from a plain program's by a relative error of at most 0.0031.
Values may be sent and summed in bfloat16 or wider, within the bound.
A program may use at most 64 MiB of HBM per device.

v0:
```python
import math
import jax
import jax.numpy as jnp
from jax import lax
from jax.sharding import PartitionSpec as P


def energy_field(strains, moduli):
    strain_xx = strains[0].astype(jnp.float32)
    strain_yy = strains[1].astype(jnp.float32)
    strain_zz = strains[2].astype(jnp.float32)
    strain_xy = strains[3].astype(jnp.float32)
    strain_yz = strains[4].astype(jnp.float32)
    strain_xz = strains[5].astype(jnp.float32)
    lame_first = moduli[0][None, :]
    shear_mod = moduli[1][None, :]
    strain_trace = strain_xx + strain_yy + strain_zz
    mean_strain = strain_trace / 3.0
    dev_xx = strain_xx - mean_strain
    dev_yy = strain_yy - mean_strain
    dev_zz = strain_zz - mean_strain
    dev_square = (
        dev_xx * dev_xx
        + dev_yy * dev_yy
        + dev_zz * dev_zz
        + 2.0 * (strain_xy * strain_xy + strain_yz * strain_yz + strain_xz * strain_xz)
    ) / 6.0
    dev_norm = jnp.sqrt(dev_square)
    dev_det = (
        dev_xx * (dev_yy * dev_zz - strain_yz * strain_yz)
        - strain_xy * (strain_xy * dev_zz - strain_yz * strain_xz)
        + strain_xz * (strain_xy * strain_yz - dev_yy * strain_xz)
    )
    sine_part = jnp.sqrt(
        jnp.maximum(4.0 * dev_square * dev_square * dev_square - dev_det * dev_det, 0.0)
    )
    angle_third = jnp.arctan2(sine_part, dev_det) / 3.0
    positive_trace = jnp.maximum(strain_trace, 0.0)
    density = 0.5 * lame_first * positive_trace * positive_trace
    for order in range(3):
        principal = mean_strain + 2.0 * dev_norm * jnp.cos(
            angle_third - 2.0 * math.pi * order / 3.0
        )
        positive = jnp.maximum(principal, 0.0)
        density = density + shear_mod * positive * positive
    return density.astype(jnp.bfloat16)


def per_device(strains, moduli, range_test, corange_test, core_left, core_right):
    energy = energy_field(strains, moduli)
    snap_rows = energy.shape[0]
    range_part = jnp.dot(energy, range_test, preferred_element_type=jnp.float32)
    cross_part = lax.dot_general(
        energy, core_right, (((1,), (1,)), ((), ())), preferred_element_type=jnp.float32
    )
    range_sketch = lax.psum(range_part, "pts")
    core_share = jnp.dot(core_left, cross_part, precision=lax.Precision.HIGHEST)
    core_sketch = lax.psum(core_share, ("snap", "pts"))
    own_cols = lax.dynamic_slice_in_dim(
        corange_test, lax.axis_index("snap") * snap_rows, snap_rows, 1
    )
    corange_sketch = lax.psum_scatter(
        jnp.dot(own_cols, energy, preferred_element_type=jnp.float32),
        "snap",
        scatter_dimension=0,
        tiled=True,
    )
    return (range_sketch, corange_sketch, core_sketch)


def solution(mesh):
    in_specs = (
        P(None, "snap", "pts"),
        P(None, "pts"),
        P("pts", None),
        P(),
        P(None, "snap"),
        P(None, "pts"),
    )
    out_specs = (P("snap", None), P("snap", "pts"), P())
    return jax.shard_map(
        per_device, mesh=mesh, in_specs=in_specs, out_specs=out_specs, check_vma=False
    )
```

profile of v0, /device:TPU:0, one launch (start us, length us, event | category | flops | bytes accessed | tf_op | source)
XLA Modules:
  0.0 557.0 jit_solution(8219614878723953401)
XLA Ops:
  8.0 0.0 copy-start
  8.0 0.0 all-reduce.5.cloned.1.call-start
  8.1 0.9 slice_multiply_fusion
  9.0 0.0 copy-start.1
  9.0 31.8 %fusion.11 = bf16[128,4096]{1,0:T(8,128)(2,1)S(1)} fusion(bf16[6,128,4096]{2,1,0:T(8,128)(2,1)} %param.6, f32[4096]{0:T(1024)S(1)} %bitcast.30, f32[4096]{0:T(1024)S(1)} %bitcast.29), kind=kLoop, calls=%fused_computation.30 | loop fusion | flops 36700160 | bytes 7372800 | tf_op jit(solution)/shard_map/convert_element_type | solution.py:46
  40.9 0.0 copy-done.1
  40.9 0.0 copy-start.2
  40.9 1.5 fusion.27
  42.4 0.0 copy-done.2
  42.4 2.0 convolution_bitcast_fusion
  44.4 0.0 all-reduce.5.cloned.1.call-update
  44.5 0.0 all-reduce.3.cloned.1.call-start
  44.5 0.0 copy-done
  44.5 1.1 fusion.26
  45.6 0.0 all-reduce.3.cloned.1.call-update
  45.7 0.0 reduce-scatter.2.cloned.1.call-start
  45.7 3.5 fusion.23
  49.2 0.0 reduce-scatter.2.cloned.1.call-update
  49.2 170.6 %all-reduce.5.cloned.1.call-done = f32[512,512]{0,1:T(8,128)} async-done(((f32[512,512]{0,1:T(8,128)}), f32[512,512]{0,1:T(8,128)}) %all-reduce.5.cloned.1.call-update) | async-done | bytes 1048592 | tf_op jit(solution)/shard_map/psum | solution.py:58
  219.8 2.5 copy.9
  222.3 325.7 %all-reduce.3.cloned.1.call-done = f32[128,256]{1,0:T(8,128)} async-done(((f32[128,256]{1,0:T(8,128)}), f32[128,256]{1,0:T(8,128)}) %all-reduce.3.cloned.1.call-update) | async-done | bytes 131088 | tf_op jit(solution)/shard_map/psum | solution.py:56
  548.0 0.0 reduce-scatter.2.cloned.1.call-done
  548.0 1.6 copy.12
Async XLA Ops:
  8.0 36.5 %copy-start = (bf16[4096,256]{1,0:T(8,128)(2,1)S(1)}, bf16[4096,256]{1,0:T(8,128)(2,1)}, u32[]{:S(2)}) copy-start(bf16[4096,256]{1,0:T(8,128)(2,1)} %param.8) | copy-start | bytes 6291460
  8.0 211.8 %all-reduce.5.cloned.1.call-start = ((), (), s32[]{:S(2)}) async-start(), calls=%async_computation.3 | async-start | bytes 2097152 | tf_op jit(solution)/shard_map/psum | solution.py:58
  9.0 31.9 %copy-start.1 = (bf16[512,4096]{1,0:T(8,128)(2,1)S(1)}, bf16[512,4096]{1,0:T(8,128)(2,1)}, u32[]{:S(2)}) copy-start(bf16[512,4096]{1,0:T(8,128)(2,1)} %param.11) | copy-start | bytes 12582916
  40.9 1.6 copy-start.2
  44.5 503.6 %all-reduce.3.cloned.1.call-start = ((), (), s32[]{:S(2)}) async-start(), calls=%async_computation.1 | async-start | bytes 262144 | tf_op jit(solution)/shard_map/psum | solution.py:56
  45.7 502.4 %reduce-scatter.2.cloned.1.call-start = ((), (), s32[]{:S(2)}) async-start(), calls=%async_computation.2 | async-start | bytes 5242880 | tf_op jit(solution)/shard_map/reduce_scatter | solution.py:62
Sparse Core Ops, SparseCore 0:
  44.6 175.1 all-reduce.4
  222.8 325.1 all-reduce.2
Sparse Core Ops, SparseCore 1:
  49.3 47.8 reduce-scatter.1
where the time goes:
time: 557 us
  waiting for transfers between devices  496 us (89%)
  other arithmetic  32.8 us (6%)
  between operations  15.6 us (3%)
  matrix products  8.11 us (1%)
    psum x1, waiting for transfers between devices, per_device(): range_sketch = lax.psum(range_part, 'pts')  326 us
    psum x1, waiting for transfers between devices, per_device(): core_sketch = lax.psum(core_share, ('snap', 'pts'))  171 us
    convert_element_type x1, other arithmetic, energy_field(): return density.astype(jnp.bfloat16)  31.8 us
  transfers between devices with their start and end apart: 3, of which 2 were waited for; matrix products, arithmetic and copies ran while one was open for 1% of the time, Pallas kernels for 0%

commit v1 on v0

--- a/solution.py
+++ b/solution.py
@@ -55,7 +55,7 @@
     )
     range_sketch = lax.psum(range_part, "pts")
     core_share = jnp.dot(core_left, cross_part, precision=lax.Precision.HIGHEST)
-    core_sketch = lax.psum(core_share, ("snap", "pts"))
+    core_sketch = lax.psum(lax.psum(core_share, "pts"), "snap")
     own_cols = lax.dynamic_slice_in_dim(
         corange_test, lax.axis_index("snap") * snap_rows, snap_rows, 1
     )

time: 557 us -> 498 us (0.89)
  waiting for transfers between devices: 496 us -> 438 us
    psum x1, waiting for transfers between devices: 171 us -> 38.9 us  [per_device(): core_sketch = lax.psum(lax.psum(core_share, 'pts'), 'snap')]
    reduce_scatter x1, waiting for transfers between devices: 0.01 us -> 46.9 us  [per_device(): lax.psum_scatter(jnp.dot(own_cols, energy, preferred_element_type=jnp.flo...]
    psum x1, waiting for transfers between devices: 326 us -> 352 us  [per_device(): range_sketch = lax.psum(range_part, 'pts')]
  transfers between devices with their start and end apart: 3 -> 3, of which waited for: 2 -> 3; matrix products, arithmetic and copies ran while one was open for 1% -> 1% of each run, Pallas kernels for 0% -> 0%
where the time goes in v1:
time: 498 us; the launch traced here: 496 us
  waiting for transfers between devices  438 us (88%)
  other arithmetic  32.8 us (7%)
  between operations  13.8 us (3%)
  matrix products  8.11 us (2%)
    psum x1, waiting for transfers between devices, per_device(): range_sketch = lax.psum(range_part, 'pts')  352 us
    reduce_scatter x1, waiting for transfers between devices, per_device(): lax.psum_scatter(jnp.dot(own_cols, energy, preferred_element_type=jnp.flo...  46.9 us
    psum x1, waiting for transfers between devices, per_device(): core_sketch = lax.psum(lax.psum(core_share, 'pts'), 'snap')  38.9 us
    convert_element_type x1, other arithmetic, energy_field(): return density.astype(jnp.bfloat16)  31.8 us
  transfers between devices with their start and end apart: 3, of which 3 were waited for; matrix products, arithmetic and copies ran while one was open for 1% of the time, Pallas kernels for 0%

profile of v1, /device:TPU:0, one launch (start us, length us, event | category | flops | bytes accessed | tf_op | source)
XLA Modules:
  0.0 496.4 jit_solution(10489692461443247661)
XLA Ops:
  7.2 0.0 copy-start
  7.2 0.0 all-reduce.6.cloned.1.call-start
  7.2 0.9 slice_multiply_fusion
  8.2 0.0 copy-start.1
  8.2 31.8 %fusion.11 = bf16[128,4096]{1,0:T(8,128)(2,1)S(1)} fusion(bf16[6,128,4096]{2,1,0:T(8,128)(2,1)} %param.6, f32[4096]{0:T(1024)S(1)} %bitcast.30, f32[4096]{0:T(1024)S(1)} %bitcast.29), kind=kLoop, calls=%fused_computation.30 | loop fusion | flops 36700160 | bytes 7372800 | tf_op jit(solution)/shard_map/convert_element_type | solution.py:46
  40.0 0.0 copy-done.1
  40.1 1.5 fusion.27
  41.6 0.0 copy-done
  41.6 0.0 copy-start.2
  41.6 1.1 fusion.26
  42.7 0.0 copy-done.2
  42.7 2.0 convolution_bitcast_fusion
  44.7 0.0 all-reduce.6.cloned.1.call-update
  44.7 0.0 all-reduce.4.cloned.1.call-start
  44.8 352.5 %all-reduce.6.cloned.1.call-done = (f32[128,256]{1,0:T(8,128)}, f32[512,512]{0,1:T(8,128)}) async-done(((f32[128,256]{1,0:T(8,128)}, f32[512,512]{0,1:T(8,128)}), (f32[128,256]{1,0:T(8,128)}, f32[512,512]{0,1:T(8,128)})) %all-reduce.6.cloned.1.call-update) | async-done | bytes 1179664 | tf_op jit(solution)/shard_map/psum | solution.py:56
  397.3 0.0 all-reduce.4.cloned.1.call-update
  397.3 0.0 reduce-scatter.2.cloned.1.call-start
  397.3 3.5 fusion.23
  400.8 0.0 reduce-scatter.2.cloned.1.call-update
  400.8 0.0 copy-start.3
  400.8 38.9 %all-reduce.4.cloned.1.call-done = f32[512,512]{0,1:T(8,128)} async-done(((f32[512,512]{0,1:T(8,128)}), f32[512,512]{0,1:T(8,128)}) %all-reduce.4.cloned.1.call-update) | async-done | bytes 1048592 | tf_op jit(solution)/shard_map/psum | solution.py:58
  439.7 2.5 copy.9
  442.3 46.9 %reduce-scatter.2.cloned.1.call-done = f32[64,4096]{1,0:T(8,128)} async-done(((f32[256,4096]{1,0:T(8,128)}), f32[64,4096]{1,0:T(8,128)}) %reduce-scatter.2.cloned.1.call-update) | async-done | bytes 1048592 | tf_op jit(solution)/shard_map/reduce_scatter | solution.py:62
  489.2 0.0 copy-done.3
  489.2 0.7 copy.13
Async XLA Ops:
  7.2 34.4 %copy-start = (bf16[4096,256]{1,0:T(8,128)(2,1)S(1)}, bf16[4096,256]{1,0:T(8,128)(2,1)}, u32[]{:S(2)}) copy-start(bf16[4096,256]{1,0:T(8,128)(2,1)} %param.8) | copy-start | bytes 6291460
  7.2 390.1 %all-reduce.6.cloned.1.call-start = ((), (), s32[]{:S(2)}) async-start(), calls=%async_computation.3 | async-start | bytes 2359296 | tf_op jit(solution)/shard_map/psum | solution.py:56
  8.2 31.9 %copy-start.1 = (bf16[512,4096]{1,0:T(8,128)(2,1)S(1)}, bf16[512,4096]{1,0:T(8,128)(2,1)}, u32[]{:S(2)}) copy-start(bf16[512,4096]{1,0:T(8,128)(2,1)} %param.11) | copy-start | bytes 12582916
  41.6 1.1 copy-start.2
  44.7 395.0 %all-reduce.4.cloned.1.call-start = ((), (), s32[]{:S(2)}) async-start(), calls=%async_computation.2 | async-start | bytes 2097152 | tf_op jit(solution)/shard_map/psum | solution.py:58
  397.3 91.9 %reduce-scatter.2.cloned.1.call-start = ((), (), s32[]{:S(2)}) async-start(), calls=%async_computation.1 | async-start | bytes 5242880 | tf_op jit(solution)/shard_map/reduce_scatter | solution.py:62
  400.8 88.4 %copy-start.3 = (f32[128,256]{1,0:T(8,128)S(1)}, f32[128,256]{1,0:T(8,128)}, u32[]{:S(2)}) copy-start(f32[128,256]{1,0:T(8,128)} %get-tuple-element.10) | copy-start | bytes 393220
Sparse Core Ops, SparseCore 0:
  44.9 352.3 all-reduce.5
  399.8 39.9 all-reduce.3
  442.7 46.4 reduce-scatter.1
